TPU v7x, 256 devices: a whole 4x4x8 slice. The times are simulated.
256 devices in a mesh: row: 8 (over y, core), col: 32 (over z, x).
Axes of the slice: x: 4, y: 4, z: 8, core: 2. Of those that a mesh axis runs over, the one named last changes fastest.
Arguments:
- row_points: float32 [64, 16384], P(None, 'row'), may hold values from -6 to 6
- panel_points: float32 [64, 1024], P(None, 'col'), may hold values from -6 to 6
- scales: float32 [64], replicated, may hold values from 0.005 to 0.03
Outputs:
- diag_factor: float32 [1024, 1024], P('row', 'col')
- panel_factor_t: float32 [1024, 16384], P('col', 'row')
- updated_ahead_t: float32 [1024, 16384], P('col', 'row')
All inputs are finite; a program needn't handle non-finite values.
Results may differ from a plain program's by a relative error of at most 0.0003.
Values sent between devices are 32-bit elements; how exact they have to be, the bound alone decides.
No kernel may reach another device: no remote copies, remote signals or barrier semaphores. Data moves between devices by JAX's collectives and lax.ppermute only.
A program may use at most 128 MiB of HBM per device.

v0:
```python
import jax
import jax.numpy as jnp
from jax import lax
from jax.sharding import PartitionSpec as P

B = 1024
RIDGE = 0.5


def spread(block, axis, holder):
    block = jnp.where(lax.axis_index(axis) == holder, block, jnp.zeros_like(block))
    return lax.psum(block, axis)


def kernel_block(sources, targets, scales):
    weighted = sources * scales[:, None]
    source_sq = jnp.sum(weighted * sources, axis=0)
    target_sq = jnp.sum(targets * targets * scales[:, None], axis=0)
    cross = lax.dot_general(
        weighted,
        targets,
        (((0,), (0,)), ((), ())),
        precision=lax.Precision.HIGHEST,
        preferred_element_type=jnp.float32,
    )
    return jnp.exp(2.0 * cross - source_sq[:, None] - target_sq[None, :])


def times_left(matrix, pieces):
    return jnp.dot(
        matrix, pieces, precision=lax.Precision.HIGHEST, preferred_element_type=jnp.float32
    )


def transposed_times(matrix, pieces):
    return lax.dot_general(
        matrix,
        pieces,
        (((0,), (0,)), ((), ())),
        precision=lax.Precision.HIGHEST,
        preferred_element_type=jnp.float32,
    )


def body(row_points, panel_points, scales):
    n_col = lax.axis_size("col")
    n_row = lax.axis_size("row")
    col_index = lax.axis_index("col")
    row_index = lax.axis_index("row")
    col_share = B // n_col
    row_share = B // n_row
    rows_dev = row_points.shape[1]
    all_panel = lax.all_gather(panel_points, "col", axis=1, tiled=True)
    first_col = col_index * col_share
    root_row = first_col // rows_dev
    local_look = lax.dynamic_slice_in_dim(row_points, first_col % rows_dev, col_share, 1)
    look_points = spread(local_look, "row", root_row)
    identity = jnp.eye(B, dtype=jnp.float32)
    diag_block = kernel_block(all_panel, all_panel, scales) + RIDGE * identity
    diag_full = jnp.linalg.cholesky(diag_block)
    inverse = lax.linalg.triangular_solve(diag_full, identity, left_side=True, lower=True)
    own_inverse = lax.dynamic_slice_in_dim(inverse, first_col, col_share, 0)
    look_kernel = kernel_block(all_panel, look_points, scales)
    look_factor = times_left(inverse, look_kernel)
    look_rows = kernel_block(look_points, row_points, scales)
    own_kernel = kernel_block(panel_points, row_points, scales)
    panel_tile = times_left(own_inverse, lax.all_gather(own_kernel, "col", axis=0, tiled=True))
    reduction = transposed_times(look_factor, lax.all_gather(panel_tile, "col", axis=0, tiled=True))
    updated = look_rows - reduction
    diag_tile = lax.dynamic_slice(
        diag_full, (row_index * row_share, first_col), (row_share, col_share)
    )
    return (diag_tile, panel_tile, updated)


def solution(mesh):
    return jax.shard_map(
        body,
        mesh=mesh,
        in_specs=(P(None, "row"), P(None, "col"), P()),
        out_specs=(P("row", "col"), P("col", "row"), P("col", "row")),
        check_vma=False,
    )
```

profile of v0, /device:TPU:1, one launch (start us, length us, event | category | flops | bytes accessed | tf_op | source)
XLA Modules:
  0.0 573.6 jit_solution(7809796819884871075)
XLA Ops:
  8.1 23.8 %psum.7 = f32[64,32]{0,1:T(8,128)S(1)} all-reduce(f32[64,32]{0,1:T(8,128)S(1)} %broadcast_select_fusion), channel_id=1, replica_groups=mesh['row'=8,'col'=32] {'row'}, use_global_device_ids=true, to_apply=%region_20.21 | all-reduce | flops 2048 | bytes 16384 | tf_op jit(solution)/shard_map/psum | solution.py:12
  36.3 42.3 %all_gather.9 = f32[64,1024]{0,1:T(8,128)S(1)} all-gather(f32[64,32]{0,1:T(8,128)} %param.4), channel_id=1, replica_groups=mesh['row'=8,'col'=32] {'col'}, dimensions={1}, use_global_device_ids=true | all-gather | bytes 270336 | tf_op jit(solution)/shard_map/all_gather | solution.py:53
  88.4 5.5 copy.6
  100.8 11.7 %cholesky.222 = f32[128,128]{1,0:T(8,128)S(1)} custom-call(f32[128,128]{1,0:T(8,128)S(1)} %cholesky.577), custom_call_target="Cholesky" | custom-call | tf_op jit(solution)/shard_map/jit(cholesky)/cholesky | solution.py:60
  112.5 9.8 %custom-call.62 = f32[1,128,128]{1,2,0:T(8,128)S(1)} custom-call(f32[1,128,128]{2,1,0:T(8,128)S(1)} %get-tuple-element.77), custom_call_target="InvertDiagBlocksLowerTriangular" | custom-call | tf_op jit(solution)/shard_map/jit(cholesky)/cholesky | solution.py:60
  128.6 11.7 %cholesky.243 = f32[128,128]{1,0:T(8,128)S(1)} custom-call(f32[128,128]{1,0:T(8,128)S(1)} %cholesky.581), custom_call_target="Cholesky" | custom-call | tf_op jit(solution)/shard_map/jit(cholesky)/cholesky | solution.py:60
  141.8 10.0 %custom-call.63 = f32[1,128,128]{1,2,0:T(8,128)S(1)} custom-call(f32[1,128,128]{2,1,0:T(8,128)S(1)} %get-tuple-element.74), custom_call_target="InvertDiagBlocksLowerTriangular" | custom-call | tf_op jit(solution)/shard_map/jit(cholesky)/cholesky | solution.py:60
  155.1 11.7 %cholesky.466 = f32[128,128]{1,0:T(8,128)S(1)} custom-call(f32[128,128]{1,0:T(8,128)S(1)} %cholesky.586), custom_call_target="Cholesky" | custom-call | tf_op jit(solution)/shard_map/jit(cholesky)/cholesky | solution.py:60
  167.5 9.8 %custom-call.64 = f32[1,128,128]{1,2,0:T(8,128)S(1)} custom-call(f32[1,128,128]{2,1,0:T(8,128)S(1)} %get-tuple-element.71), custom_call_target="InvertDiagBlocksLowerTriangular" | custom-call | tf_op jit(solution)/shard_map/jit(cholesky)/cholesky | solution.py:60
  180.9 12.1 %cholesky.485 = f32[128,128]{1,0:T(8,128)S(1)} custom-call(f32[128,128]{1,0:T(8,128)S(1)} %cholesky.591), custom_call_target="Cholesky" | custom-call | tf_op jit(solution)/shard_map/jit(cholesky)/cholesky | solution.py:60
  193.6 9.8 %custom-call.65 = f32[1,128,128]{1,2,0:T(8,128)S(1)} custom-call(f32[1,128,128]{2,1,0:T(8,128)S(1)} %get-tuple-element.68), custom_call_target="InvertDiagBlocksLowerTriangular" | custom-call | tf_op jit(solution)/shard_map/jit(cholesky)/cholesky | solution.py:60
  206.9 11.7 %cholesky.504 = f32[128,128]{1,0:T(8,128)S(1)} custom-call(f32[128,128]{1,0:T(8,128)S(1)} %cholesky.596), custom_call_target="Cholesky" | custom-call | tf_op jit(solution)/shard_map/jit(cholesky)/cholesky | solution.py:60
  219.2 9.8 %custom-call.66 = f32[1,128,128]{1,2,0:T(8,128)S(1)} custom-call(f32[1,128,128]{2,1,0:T(8,128)S(1)} %get-tuple-element.65), custom_call_target="InvertDiagBlocksLowerTriangular" | custom-call | tf_op jit(solution)/shard_map/jit(cholesky)/cholesky | solution.py:60
  232.5 11.7 %cholesky.524 = f32[128,128]{1,0:T(8,128)S(1)} custom-call(f32[128,128]{1,0:T(8,128)S(1)} %cholesky.601), custom_call_target="Cholesky" | custom-call | tf_op jit(solution)/shard_map/jit(cholesky)/cholesky | solution.py:60
  244.9 9.8 %custom-call.67 = f32[1,128,128]{1,2,0:T(8,128)S(1)} custom-call(f32[1,128,128]{2,1,0:T(8,128)S(1)} %get-tuple-element.62), custom_call_target="InvertDiagBlocksLowerTriangular" | custom-call | tf_op jit(solution)/shard_map/jit(cholesky)/cholesky | solution.py:60
  257.7 11.7 %cholesky.544 = f32[128,128]{1,0:T(8,128)S(1)} custom-call(f32[128,128]{1,0:T(8,128)S(1)} %cholesky.606), custom_call_target="Cholesky" | custom-call | tf_op jit(solution)/shard_map/jit(cholesky)/cholesky | solution.py:60
  270.1 10.0 %custom-call.68 = f32[1,128,128]{1,2,0:T(8,128)S(1)} custom-call(f32[1,128,128]{2,1,0:T(8,128)S(1)} %get-tuple-element.59), custom_call_target="InvertDiagBlocksLowerTriangular" | custom-call | tf_op jit(solution)/shard_map/jit(cholesky)/cholesky | solution.py:60
  282.7 11.7 %cholesky.562 = f32[128,128]{1,0:T(8,128)S(1)} custom-call(f32[128,128]{1,0:T(8,128)S(1)} %convolution_subtract_fusion.11), custom_call_target="Cholesky" | custom-call | tf_op jit(solution)/shard_map/jit(cholesky)/cholesky | solution.py:60
  304.8 6.6 %fusion = (f32[1024,1024]{1,0:T(8,128)}, f32[1024,1024]{1,0:T(8,128)}) fusion(f32[1024,1024]{1,0:T(8,128)} %get-tuple-element.57, pred[]{:T(512)S(6)} %cholesky.576), kind=kLoop, calls=%fused_computation.8 | loop fusion | flops 4194304 | bytes 12582913 | tf_op jit(solution)/shard_map/triangular_solve | solution.py:61
  311.4 23.2 %while.1 = (s32[]{:T(128)}, f32[1024,1024]{1,0:T(8,128)}, s32[8,2]{0,1:T(2,128)S(1)}, f32[8,128,128]{2,1,0:T(8,128)S(1)}, s32[]{:T(128)}) while((s32[]{:T(128)}, f32[1024,1024]{1,0:T(8,128)}, s32[8,2]{0,1:T(2,128)S(1)}, f32[8,128,128]{2,1,0:T(8,128)S(1)}, s32[]{:T(128)}) %tuple.65), condition=%wide.while_cond, body=%wide.while_body.sunk | while | flops 2 | bytes 131181 | solution.py:61
  334.6 79.0 %custom-call.69 = f32[8,128,128]{1,2,0:T(8,128)S(1)} custom-call(f32[8,128,128]{2,1,0:T(8,128)S(1)} %get-tuple-element.10), custom_call_target="InvertDiagBlocksLowerTriangular" | custom-call | tf_op jit(solution)/shard_map/triangular_solve | solution.py:61
  442.5 9.0 %fusion.68 = f32[32,2048]{1,0:T(8,128)} fusion(f32[1024,2048]{1,0:T(8,128)} %all-gather.3.cloned.1.call-done, f32[1024,1024]{1,0:T(8,128)} %convolution_dynamic-update-slice_fusion, s32[]{:T(128)S(6)} %select_n.35), kind=kOutput, calls=%fused_computation.97 | convolution fusion | flops 805306368 | bytes 8781828 | tf_op jit(solution)/shard_map/dot_general | solution.py:30
  459.0 99.2 %all-gather.5.cloned.1.call-done = f32[1024,2048]{1,0:T(8,128)} async-done(((f32[32,2048]{1,0:T(8,128)}), f32[1024,2048]{1,0:T(8,128)}) %all-gather.5.cloned.1.call-update) | async-done | bytes 8388624 | tf_op jit(solution)/shard_map/all_gather | solution.py:68
  558.2 7.2 %fusion.98 = f32[32,2048]{1,0:T(8,128)S(1)} fusion(f32[1024,32]{1,0:T(8,128)S(1)} %fusion.97, f32[1024,2048]{1,0:T(8,128)} %all-gather.5.cloned.1.call-done), kind=kOutput, calls=%fused_computation.199 | convolution fusion | flops 805306368 | bytes 8781824 | tf_op jit(solution)/shard_map/dot_general | solution.py:36
  (111 shorter events, 117.9 us)
Async XLA Ops:
  7.2 435.4 %all-gather.3.cloned.1.call-start = ((), (), s32[]{:S(2)}) async-start(), calls=%async_computation | async-start | bytes 8650752 | tf_op jit(solution)/shard_map/all_gather | solution.py:67
  36.2 522.0 %all-gather.5.cloned.1.call-start = ((), (), s32[]{:S(2)}) async-start(), calls=%async_computation.1 | async-start | bytes 8650752 | tf_op jit(solution)/shard_map/all_gather | solution.py:68
  83.7 2.0 copy-start
  98.8 2.0 copy-start.1
  442.5 10.7 %copy-start.3 = (f32[64]{0:T(128)S(1)}, f32[64]{0:T(128)}, u32[]{:S(2)}) copy-start(f32[64]{0:T(128)} %param.5) | copy-start | bytes 772
  459.0 106.4 %copy-start.2 = (f32[64,2048]{1,0:T(8,128)S(1)}, f32[64,2048]{1,0:T(8,128)}, u32[]{:S(2)}) copy-start(f32[64,2048]{1,0:T(8,128)} %param.3) | copy-start | bytes 1572868
Sparse Core Ops, SparseCore 0:
  36.4 101.4 all-gather.2
  451.7 106.4 all-gather.4
where the time goes:
time: 581 us; the launch traced here: 574 us
  other arithmetic  269 us (46%)
  waiting for transfers between devices  99.2 us (17%)
  matrix products  80.5 us (14%)
  blocking collectives  66.1 us (11%)
  local copies, waits for them, and re-layouts  38.5 us (7%)
  between operations  19.8 us (3%)
    another operation x30, other arithmetic, body(): diag_full = jnp.linalg.cholesky(diag_block)  172 us
    all_gather x1, waiting for transfers between devices, body(): lax.all_gather(panel_tile, 'col', axis=0, tiled=True)  99.2 us
    another operation x3, other arithmetic, body(): lax.linalg.triangular_solve(diag_full, identity, left_side=True, lower=True)  85.6 us
    all_gather x1, blocking collectives, body(): all_panel = lax.all_gather(panel_points, 'col', axis=1, tiled=True)  42.3 us
    another operation x15, matrix products, body(): lax.linalg.triangular_solve(diag_full, identity, left_side=True, lower=True)  28.1 us
    psum x1, blocking collectives, spread(): return lax.psum(block, axis)  23.8 us
    another operation x24, local copies, waits for them, and re-layouts  23 us
    another operation x14, matrix products, body(): diag_full = jnp.linalg.cholesky(diag_block)  23 us
  transfers between devices with their start and end apart: 2, of which 1 were waited for; matrix products, arithmetic and copies ran while one was open for 63% of the time, Pallas kernels for 0%

commit v1 on v0

--- a/solution.py
+++ b/solution.py
@@ -50,7 +50,10 @@
     col_share = B // n_col
     row_share = B // n_row
     rows_dev = row_points.shape[1]
-    all_panel = lax.all_gather(panel_points, "col", axis=1, tiled=True)
+    count = lax.axis_size("col")
+    tiles = jnp.stack([panel_points for _ in range(count)])
+    tiles = lax.all_to_all(tiles, "col", split_axis=0, concat_axis=0)
+    all_panel = jnp.concatenate(tiles, axis=1)
     first_col = col_index * col_share
     root_row = first_col // rows_dev
     local_look = lax.dynamic_slice_in_dim(row_points, first_col % rows_dev, col_share, 1)

time: 581 us -> 554 us (0.954)
  blocking collectives: 66.1 us -> 23.8 us
  starting transfers between devices: 0.08 us -> 11.1 us
    all_gather x1 -> x0, blocking collectives: 42.3 us -> none  [body(): all_panel = lax.all_gather(panel_points, 'col', axis=1, tiled=True)]
    all_to_all x0 -> x1, starting transfers between devices: none -> 11 us  [body(): tiles = lax.all_to_all(tiles, 'col', split_axis=0, concat_axis=0)]
    all_gather x1, waiting for transfers between devices: 99.2 us -> 90 us  [body(): lax.all_gather(panel_tile, 'col', axis=0, tiled=True)]
    all_to_all x0 -> x1, waiting for transfers between devices: none -> 7.54 us  [body(): tiles = lax.all_to_all(tiles, 'col', split_axis=0, concat_axis=0)]
  transfers between devices with their start and end apart: 2 -> 3, of which waited for: 1 -> 2; matrix products, arithmetic and copies ran while one was open for 63% -> 67% of each run, Pallas kernels for 0% -> 0%
where the time goes in v1:
time: 554 us; the launch traced here: 546 us
  other arithmetic  272 us (49%)
  waiting for transfers between devices  97.6 us (18%)
  matrix products  80.1 us (14%)
  local copies, waits for them, and re-layouts  41.1 us (7%)
  blocking collectives  23.8 us (4%)
  between operations  19.9 us (4%)
  starting transfers between devices  11.1 us (2%)
    another operation x30, other arithmetic, body(): diag_full = jnp.linalg.cholesky(diag_block)  172 us
    all_gather x1, waiting for transfers between devices, body(): lax.all_gather(panel_tile, 'col', axis=0, tiled=True)  90 us
    another operation x3, other arithmetic, body(): lax.linalg.triangular_solve(diag_full, identity, left_side=True, lower=True)  85.6 us
    another operation x15, matrix products, body(): lax.linalg.triangular_solve(diag_full, identity, left_side=True, lower=True)  28.4 us
    psum x1, blocking collectives, spread(): return lax.psum(block, axis)  23.8 us
    another operation x24, local copies, waits for them, and re-layouts  23 us
    another operation x14, matrix products, body(): diag_full = jnp.linalg.cholesky(diag_block)  22.9 us
    dot_general x2, matrix products, times_left(): jnp.dot(matrix, pieces, precision=lax.Precision.HIGHEST, preferred_elemen...  14.2 us
  transfers between devices with their start and end apart: 3, of which 2 were waited for; matrix products, arithmetic and copies ran while one was open for 67% of the time, Pallas kernels for 0%

profile of v1, /device:TPU:1, one launch (start us, length us, event | category | flops | bytes accessed | tf_op | source)
XLA Modules:
  0.0 545.6 jit_solution(8322912477117681436)
XLA Ops:
  8.1 23.8 %psum.7 = f32[64,32]{0,1:T(8,128)S(1)} all-reduce(f32[64,32]{0,1:T(8,128)S(1)} %broadcast_select_fusion), channel_id=1, replica_groups=mesh['row'=8,'col'=32] {'row'}, use_global_device_ids=true, to_apply=%region_20.21 | all-reduce | flops 2048 | bytes 16384 | tf_op jit(solution)/shard_map/psum | solution.py:12
  38.1 11.0 %all-to-all-start = ((f32[32,1,2048]{2,1,0:T(1,128)}), f32[32,1,2048]{2,1,0:T(1,128)S(1)}, u32[]{:S(2)}, u32[]{:S(2)}) async-start(f32[32,1,2048]{2,1,0:T(1,128)} %reshape.131), calls=%async_computation | async-start | bytes 524288 | tf_op jit(solution)/shard_map/all_to_all | solution.py:55
  52.0 7.5 %all-to-all-done = f32[32,1,2048]{2,1,0:T(1,128)S(1)} async-done(((f32[32,1,2048]{2,1,0:T(1,128)}), f32[32,1,2048]{2,1,0:T(1,128)S(1)}, u32[]{:S(2)}, u32[]{:S(2)}) %all-to-all-start) | async-done | bytes 262176 | tf_op jit(solution)/shard_map/all_to_all | solution.py:55
  82.4 11.7 %cholesky.222 = f32[128,128]{1,0:T(8,128)S(1)} custom-call(f32[128,128]{1,0:T(8,128)S(1)} %cholesky.577), custom_call_target="Cholesky" | custom-call | tf_op jit(solution)/shard_map/jit(cholesky)/cholesky | solution.py:63
  94.2 9.8 %custom-call.62 = f32[1,128,128]{1,2,0:T(8,128)S(1)} custom-call(f32[1,128,128]{2,1,0:T(8,128)S(1)} %get-tuple-element.81), custom_call_target="InvertDiagBlocksLowerTriangular" | custom-call | tf_op jit(solution)/shard_map/jit(cholesky)/cholesky | solution.py:63
  110.3 11.7 %cholesky.243 = f32[128,128]{1,0:T(8,128)S(1)} custom-call(f32[128,128]{1,0:T(8,128)S(1)} %cholesky.581), custom_call_target="Cholesky" | custom-call | tf_op jit(solution)/shard_map/jit(cholesky)/cholesky | solution.py:63
  123.5 10.0 %custom-call.63 = f32[1,128,128]{1,2,0:T(8,128)S(1)} custom-call(f32[1,128,128]{2,1,0:T(8,128)S(1)} %get-tuple-element.78), custom_call_target="InvertDiagBlocksLowerTriangular" | custom-call | tf_op jit(solution)/shard_map/jit(cholesky)/cholesky | solution.py:63
  136.8 11.7 %cholesky.466 = f32[128,128]{1,0:T(8,128)S(1)} custom-call(f32[128,128]{1,0:T(8,128)S(1)} %cholesky.586), custom_call_target="Cholesky" | custom-call | tf_op jit(solution)/shard_map/jit(cholesky)/cholesky | solution.py:63
  149.2 9.8 %custom-call.64 = f32[1,128,128]{1,2,0:T(8,128)S(1)} custom-call(f32[1,128,128]{2,1,0:T(8,128)S(1)} %get-tuple-element.75), custom_call_target="InvertDiagBlocksLowerTriangular" | custom-call | tf_op jit(solution)/shard_map/jit(cholesky)/cholesky | solution.py:63
  162.5 12.1 %cholesky.485 = f32[128,128]{1,0:T(8,128)S(1)} custom-call(f32[128,128]{1,0:T(8,128)S(1)} %cholesky.591), custom_call_target="Cholesky" | custom-call | tf_op jit(solution)/shard_map/jit(cholesky)/cholesky | solution.py:63
  175.3 9.8 %custom-call.65 = f32[1,128,128]{1,2,0:T(8,128)S(1)} custom-call(f32[1,128,128]{2,1,0:T(8,128)S(1)} %get-tuple-element.72), custom_call_target="InvertDiagBlocksLowerTriangular" | custom-call | tf_op jit(solution)/shard_map/jit(cholesky)/cholesky | solution.py:63
  188.5 11.7 %cholesky.504 = f32[128,128]{1,0:T(8,128)S(1)} custom-call(f32[128,128]{1,0:T(8,128)S(1)} %cholesky.596), custom_call_target="Cholesky" | custom-call | tf_op jit(solution)/shard_map/jit(cholesky)/cholesky | solution.py:63
  200.9 9.8 %custom-call.66 = f32[1,128,128]{1,2,0:T(8,128)S(1)} custom-call(f32[1,128,128]{2,1,0:T(8,128)S(1)} %get-tuple-element.69), custom_call_target="InvertDiagBlocksLowerTriangular" | custom-call | tf_op jit(solution)/shard_map/jit(cholesky)/cholesky | solution.py:63
  214.2 11.7 %cholesky.524 = f32[128,128]{1,0:T(8,128)S(1)} custom-call(f32[128,128]{1,0:T(8,128)S(1)} %cholesky.601), custom_call_target="Cholesky" | custom-call | tf_op jit(solution)/shard_map/jit(cholesky)/cholesky | solution.py:63
  226.6 9.8 %custom-call.67 = f32[1,128,128]{1,2,0:T(8,128)S(1)} custom-call(f32[1,128,128]{2,1,0:T(8,128)S(1)} %get-tuple-element.66), custom_call_target="InvertDiagBlocksLowerTriangular" | custom-call | tf_op jit(solution)/shard_map/jit(cholesky)/cholesky | solution.py:63
  239.3 11.7 %cholesky.544 = f32[128,128]{1,0:T(8,128)S(1)} custom-call(f32[128,128]{1,0:T(8,128)S(1)} %cholesky.606), custom_call_target="Cholesky" | custom-call | tf_op jit(solution)/shard_map/jit(cholesky)/cholesky | solution.py:63
  251.7 10.0 %custom-call.68 = f32[1,128,128]{1,2,0:T(8,128)S(1)} custom-call(f32[1,128,128]{2,1,0:T(8,128)S(1)} %get-tuple-element.63), custom_call_target="InvertDiagBlocksLowerTriangular" | custom-call | tf_op jit(solution)/shard_map/jit(cholesky)/cholesky | solution.py:63
  264.3 11.7 %cholesky.562 = f32[128,128]{1,0:T(8,128)S(1)} custom-call(f32[128,128]{1,0:T(8,128)S(1)} %convolution_subtract_fusion.11), custom_call_target="Cholesky" | custom-call | tf_op jit(solution)/shard_map/jit(cholesky)/cholesky | solution.py:63
  286.4 6.6 %fusion = (f32[1024,1024]{1,0:T(8,128)}, f32[1024,1024]{1,0:T(8,128)}) fusion(f32[1024,1024]{1,0:T(8,128)} %get-tuple-element.61, pred[]{:T(512)S(6)} %cholesky.576), kind=kLoop, calls=%fused_computation.8 | loop fusion | flops 4194304 | bytes 12582913 | tf_op jit(solution)/shard_map/triangular_solve | solution.py:64
  293.0 23.2 %while.1 = (s32[]{:T(128)}, f32[1024,1024]{1,0:T(8,128)}, s32[8,2]{0,1:T(2,128)S(1)}, f32[8,128,128]{2,1,0:T(8,128)S(1)}, s32[]{:T(128)}) while((s32[]{:T(128)}, f32[1024,1024]{1,0:T(8,128)}, s32[8,2]{0,1:T(2,128)S(1)}, f32[8,128,128]{2,1,0:T(8,128)S(1)}, s32[]{:T(128)}) %tuple.67), condition=%wide.while_cond, body=%wide.while_body.sunk | while | flops 2 | bytes 131181 | solution.py:64
  316.2 79.0 %custom-call.69 = f32[8,128,128]{1,2,0:T(8,128)S(1)} custom-call(f32[8,128,128]{2,1,0:T(8,128)S(1)} %get-tuple-element.10), custom_call_target="InvertDiagBlocksLowerTriangular" | custom-call | tf_op jit(solution)/shard_map/triangular_solve | solution.py:64
  423.6 9.0 %fusion.67 = f32[32,2048]{1,0:T(8,128)} fusion(f32[1024,2048]{1,0:T(8,128)} %all-gather.3.cloned.1.call-done, f32[1024,1024]{1,0:T(8,128)} %convolution_dynamic-update-slice_fusion, s32[]{:T(128)S(6)} %select_n.35), kind=kOutput, calls=%fused_computation.97 | convolution fusion | flops 805306368 | bytes 8781828 | tf_op jit(solution)/shard_map/dot_general | solution.py:30
  440.1 90.0 %all-gather.5.cloned.1.call-done = f32[1024,2048]{1,0:T(8,128)} async-done(((f32[32,2048]{1,0:T(8,128)}), f32[1024,2048]{1,0:T(8,128)}) %all-gather.5.cloned.1.call-update) | async-done | bytes 8388624 | tf_op jit(solution)/shard_map/all_gather | solution.py:71
  530.2 7.2 %fusion.98 = f32[32,2048]{1,0:T(8,128)S(1)} fusion(f32[1024,32]{1,0:T(8,128)S(1)} %fusion.97, f32[1024,2048]{1,0:T(8,128)} %all-gather.5.cloned.1.call-done), kind=kOutput, calls=%fused_computation.201 | convolution fusion | flops 805306368 | bytes 8781824 | tf_op jit(solution)/shard_map/dot_general | solution.py:36
  (121 shorter events, 128.2 us)
Async XLA Ops:
  7.2 416.5 %all-gather.3.cloned.1.call-start = ((), (), s32[]{:S(2)}) async-start(), calls=%async_computation.1 | async-start | bytes 8650752 | tf_op jit(solution)/shard_map/all_gather | solution.py:70
  36.2 25.3 %copy-start.4 = (f32[64]{0:T(128)S(1)}, f32[64]{0:T(128)}, u32[]{:S(2)}) copy-start(f32[64]{0:T(128)} %param.5) | copy-start | bytes 772
  38.1 21.5 %all-to-all-start = ((f32[32,1,2048]{2,1,0:T(1,128)}), f32[32,1,2048]{2,1,0:T(1,128)S(1)}, u32[]{:S(2)}, u32[]{:S(2)}) async-start(f32[32,1,2048]{2,1,0:T(1,128)} %reshape.131), calls=%async_computation | async-start | bytes 524288 | tf_op jit(solution)/shard_map/all_to_all | solution.py:55
  49.1 481.1 %all-gather.5.cloned.1.call-start = ((), (), s32[]{:S(2)}) async-start(), calls=%async_computation.2 | async-start | bytes 8650752 | tf_op jit(solution)/shard_map/all_gather | solution.py:71
  65.5 2.0 copy-start
  80.5 2.0 copy-start.2
  395.2 4.7 copy-start.1
  440.1 97.3 %copy-start.3 = (f32[64,2048]{1,0:T(8,128)S(1)}, f32[64,2048]{1,0:T(8,128)}, u32[]{:S(2)}) copy-start(f32[64,2048]{1,0:T(8,128)} %param.3) | copy-start | bytes 1572868
Sparse Core Ops, SparseCore 0:
  36.4 101.7 all-gather.2
  432.8 97.3 all-gather.4
